TPU v7x, 32 devices: a whole 2x2x4 slice. The times are simulated.
32 devices in a mesh: row: 4 (over y, x), col: 8 (over z, core).
Axes of the slice: x: 2, y: 2, z: 4, core: 2. Of those that a mesh axis runs over, the one named last changes fastest.
Arguments:
- image: bfloat16 [64, 256, 768], P('row', 'col'), may hold values from -6 to 6
- conv_taps: float32 [9, 768], replicated, may hold values from -0.5 to 0.5
- w_query: bfloat16 [768, 768], replicated, may hold values from -0.21875 to 0.21875
- w_key: bfloat16 [768, 768], replicated, may hold values from -0.21875 to 0.21875
- w_value: bfloat16 [768, 768], replicated, may hold values from -0.21875 to 0.21875
- w_out: bfloat16 [768, 768], replicated, may hold values from -0.21875 to 0.21875
- grad_out: bfloat16 [64, 256, 768], P('row', 'col'), may hold values from -6 to 6
Outputs:
- grad_image: bfloat16 [64, 256, 768], P('row', 'col')
- grad_weights: float32 [768, 3072], P(None, 'col')
- grad_conv: float32 [9, 768], P(None, 'col')
All inputs are finite; a program needn't handle non-finite values.
Results may differ from a plain program's by a relative error of at most 0.022.
Values may be sent and summed in bfloat16 or wider, within the bound.
A program may use at most 128 MiB of HBM per device.

v0:
```python
from functools import partial
import math
import jax
import jax.numpy as jnp
from jax import lax
from jax.sharding import PartitionSpec as P

HEADS = 12
HD = 64
POOL = 8
EPSILON = 1e-05


def with_halo(cells, sides, width):
    for axis, dim in sides:
        count = lax.axis_size(axis)
        ends = count - 1
        head = lax.slice_in_dim(cells, 0, width, axis=dim)
        tail = lax.slice_in_dim(cells, cells.shape[dim] - width, cells.shape[dim], axis=dim)
        cells = jnp.concatenate(
            [
                lax.ppermute(tail, axis, [(i, (i + 1) % count) for i in range(ends)]),
                cells,
                lax.ppermute(head, axis, [((i + 1) % count, i) for i in range(ends)]),
            ],
            axis=dim,
        )
    return cells


def contract_first(left, right):
    return lax.dot_general(
        left, right, (((0,), (0,)), ((), ())), preferred_element_type=jnp.float32
    )


def contract_last(left, right):
    return lax.dot_general(
        left, right, (((1,), (1,)), ((), ())), preferred_element_type=jnp.float32
    )


def exact_first(left, right):
    return lax.dot_general(
        left,
        right,
        (((0,), (0,)), ((), ())),
        precision=lax.Precision.HIGHEST,
        preferred_element_type=jnp.float32,
    )


def exact_last(left, right):
    return lax.dot_general(
        left,
        right,
        (((1,), (1,)), ((), ())),
        precision=lax.Precision.HIGHEST,
        preferred_element_type=jnp.float32,
    )


def stencil(padded, taps, height, width, flipped):
    total = jnp.zeros((height, width, padded.shape[2]), jnp.float32)
    for tap_row in range(3):
        for tap_col in range(3):
            if flipped:
                window = padded[
                    2 - tap_row : 2 - tap_row + height, 2 - tap_col : 2 - tap_col + width
                ]
            else:
                window = padded[tap_row : tap_row + height, tap_col : tap_col + width]
            total = total + taps[3 * tap_row + tap_col] * window.astype(jnp.float32)
    return total


def attend(carry, inputs, key_heads, value_heads):
    grad_key, grad_value = carry
    query_block, dout_block = inputs
    softmax_scale = HD ** (-0.5)
    query_heads = query_block.reshape(-1, HEADS, HD)
    dout_heads = dout_block.reshape(-1, HEADS, HD)
    scores = (
        jnp.einsum("qhd,khd->hqk", query_heads, key_heads, preferred_element_type=jnp.float32)
        * softmax_scale
    )
    expons = jnp.exp(scores)
    probabilities = expons / jnp.sum(expons, axis=-1, keepdims=True)
    weights = probabilities.astype(jnp.bfloat16)
    attended = jnp.einsum(
        "hqk,khd->qhd", weights, value_heads, preferred_element_type=jnp.float32
    ).astype(jnp.bfloat16)
    grad_probs = jnp.einsum(
        "qhd,khd->hqk", dout_heads, value_heads, preferred_element_type=jnp.float32
    )
    deltas = jnp.einsum("qhd,qhd->hq", dout_heads, attended, preferred_element_type=jnp.float32)
    grad_scores = (probabilities * (grad_probs - deltas[:, :, None]) * softmax_scale).astype(
        jnp.bfloat16
    )
    grad_query = jnp.einsum(
        "hqk,khd->qhd", grad_scores, key_heads, preferred_element_type=jnp.float32
    ).astype(jnp.bfloat16)
    grad_key = grad_key + jnp.einsum(
        "hqk,qhd->khd", grad_scores, query_heads, preferred_element_type=jnp.float32
    )
    grad_value = grad_value + jnp.einsum(
        "hqk,qhd->khd", weights, dout_heads, preferred_element_type=jnp.float32
    )
    return (
        (grad_key, grad_value),
        (attended.reshape(query_block.shape), grad_query.reshape(query_block.shape)),
    )


def on_device(image, conv_taps, w_query, w_key, w_value, w_out, grad_out):
    height, width, channels = image.shape
    padded = with_halo(image, (("row", 0), ("col", 1)), 1)
    mixed = image.astype(jnp.float32) + stencil(padded, conv_taps, height, width, False)
    hidden = mixed.astype(jnp.bfloat16)
    flat_hidden = hidden.reshape(-1, channels)
    query = jnp.dot(flat_hidden, w_query, preferred_element_type=jnp.float32).astype(jnp.bfloat16)
    pooled = (
        hidden.astype(jnp.float32)
        .reshape(height // POOL, POOL, width // POOL, POOL, channels)
        .mean(axis=(1, 3))
    )
    centre = jnp.mean(pooled, axis=-1, keepdims=True)
    spread = jnp.mean(jnp.square(pooled - centre), axis=-1, keepdims=True)
    inverse = lax.rsqrt(spread + EPSILON)
    standard = (pooled - centre) * inverse
    normed = standard.astype(jnp.bfloat16)
    gathered = lax.all_gather(normed, "col", axis=1, tiled=True)
    pooled_rows, pooled_cols = (gathered.shape[0], gathered.shape[1])
    key_cells = gathered.reshape(-1, channels)
    keys = jnp.dot(key_cells, w_key, preferred_element_type=jnp.float32).astype(jnp.bfloat16)
    values = jnp.dot(key_cells, w_value, preferred_element_type=jnp.float32).astype(jnp.bfloat16)
    flat_grad = grad_out.reshape(-1, channels)
    dout = contract_last(flat_grad, w_out).astype(jnp.bfloat16)
    total_rows = flat_hidden.shape[0]
    block_rows = math.gcd(total_rows, 512)
    blocks = total_rows // block_rows
    key_heads = keys.reshape(-1, HEADS, HD)
    value_heads = values.reshape(-1, HEADS, HD)
    empty_grad = jnp.zeros(key_heads.shape, jnp.float32)
    carry, produced = lax.scan(
        partial(attend, key_heads=key_heads, value_heads=value_heads),
        (empty_grad, empty_grad),
        (query.reshape(blocks, block_rows, channels), dout.reshape(blocks, block_rows, channels)),
    )
    grad_key = carry[0].reshape(pooled_rows, pooled_cols, channels)
    grad_value = carry[1].reshape(pooled_rows, pooled_cols, channels)
    attended = produced[0].reshape(-1, channels)
    grad_query = produced[1].reshape(-1, channels)
    grad_wout = contract_first(attended, flat_grad)
    grad_wquery = contract_first(flat_hidden, grad_query)
    grad_hidden = contract_last(grad_query, w_query)
    key_float = w_key.astype(jnp.float32)
    value_float = w_value.astype(jnp.float32)
    flat_key = grad_key.reshape(-1, channels)
    flat_value = grad_value.reshape(-1, channels)
    cell_terms = exact_last(flat_key, key_float) + exact_last(flat_value, value_float)
    cells_float = key_cells.astype(jnp.float32)
    grad_wkey = exact_first(cells_float, flat_key)
    grad_wvalue = exact_first(cells_float, flat_value)
    grad_normed = lax.psum_scatter(
        cell_terms.reshape(pooled_rows, pooled_cols, channels).astype(jnp.bfloat16),
        "col",
        scatter_dimension=1,
        tiled=True,
    ).astype(jnp.float32)
    grad_pooled = (
        grad_normed
        - jnp.mean(grad_normed, axis=-1, keepdims=True)
        - standard * jnp.mean(grad_normed * standard, axis=-1, keepdims=True)
    ) * inverse
    spread_back = jnp.broadcast_to(
        (grad_pooled / (POOL * POOL))[:, None, :, None, :],
        (height // POOL, POOL, width // POOL, POOL, channels),
    ).reshape(height, width, channels)
    grad_mixed = (
        grad_out.astype(jnp.float32) + grad_hidden.reshape(height, width, channels) + spread_back
    )
    grad_padded = with_halo(grad_mixed.astype(jnp.bfloat16), (("row", 0), ("col", 1)), 1).astype(
        grad_mixed.dtype
    )
    grad_image = (grad_mixed + stencil(grad_padded, conv_taps, height, width, True)).astype(
        jnp.bfloat16
    )
    tap_list = []
    for tap_row in range(3):
        for tap_col in range(3):
            window = padded[tap_row : tap_row + height, tap_col : tap_col + width].astype(
                jnp.float32
            )
            tap_list.append(jnp.sum(grad_mixed * window, axis=(0, 1)))
    tap_terms = jnp.stack(tap_list, axis=0)
    weight_terms = jnp.concatenate([grad_wquery, grad_wkey, grad_wvalue, grad_wout], axis=1)
    column_sums = (
        lax.psum_scatter(
            weight_terms.astype(jnp.bfloat16), "col", scatter_dimension=1, tiled=True
        ).astype(jnp.float32),
        lax.psum_scatter(
            tap_terms.astype(jnp.bfloat16), "col", scatter_dimension=1, tiled=True
        ).astype(jnp.float32),
    )
    grad_weights, grad_conv = (
        lax.psum(column_sums[0].astype(jnp.bfloat16), "row").astype(jnp.float32),
        lax.psum(column_sums[1].astype(jnp.bfloat16), "row").astype(jnp.float32),
    )
    return (grad_image, grad_weights, grad_conv)


def solution(mesh):
    return jax.shard_map(
        on_device,
        mesh=mesh,
        in_specs=(P("row", "col", None), P(), P(), P(), P(), P(), P("row", "col", None)),
        out_specs=(P("row", "col", None), P(None, "col"), P(None, "col")),
        check_vma=False,
    )
```

profile of v0, /device:TPU:0, one launch (start us, length us, event | category | flops | bytes accessed | tf_op | source)
XLA Modules:
  0.0 293.8 jit_solution(12890035376737956254)
XLA Ops:
  8.1 4.9 %collective-permute-start = (bf16[1,32,768]{2,1,0:T(8,128)(2,1)S(1)}, bf16[1,32,768]{2,1,0:T(8,128)(2,1)S(1)}, u32[]{:S(2)}, u32[]{:S(2)}) collective-permute-start(bf16[1,32,768]{2,1,0:T(8,128)(2,1)S(1)} %get-tuple-element.78), channel_id=1, source_target_pairs={{0,8},{8,16},{16,24},{1,9},{9,17},{17,25},{2,10},{10,18},{18,26},{... | collective-permute-start | bytes 147464 | tf_op jit(solution)/shard_map/ppermute | solution.py:22
  14.3 2.4 convolution_convert_fusion.4
  16.8 2.2 collective-permute-done.1
  21.2 3.7 %collective-permute-start.2 = (bf16[18,1,768]{2,1,0:T(2,128)(2,1)}, bf16[18,1,768]{2,1,0:T(2,128)(2,1)}, u32[]{:S(2)}, u32[]{:S(2)}) collective-permute-start(bf16[18,1,768]{2,1,0:T(2,128)(2,1)} %get-tuple-element.75), channel_id=1, source_target_pairs={{0,1},{1,2},{2,3},{3,4},{4,5},{5,6},{6,7},{8,9},{9,10},{10,11},{11... | collective-permute-start | bytes 82952 | tf_op jit(solution)/shard_map/ppermute | solution.py:22
  27.7 5.4 %fusion.28 = bf16[16,32,768]{2,1,0:T(8,128)(2,1)S(1)} fusion(bf16[16,32,768]{2,1,0:T(8,128)(2,1)S(1)} %copy-done.5, bf16[1,32,768]{2,1,0:T(8,128)(2,1)} %copy-done.23, bf16[1,32,768]{2,1,0:T(8,128)(2,1)} %copy-done.22, f32[768]{0:T(1024)} %get-tuple-element.69, f32[768]{0:T(1024)} %get-tuple-element.70, f32[768]{0:T(1024)S(1)} %get-tuple-element.63, ...), kind=kLoop, calls=%fused_computation.62 | loop fusion | flops 20447232 | bytes 2638848 | tf_op jit(solution)/shard_map/convert_element_type | solution.py:119
  35.7 2.4 copy.51
  40.3 14.0 %all_gather.3 = bf16[2,32,768]{2,0,1:T(2,128)(2,1)S(1)} all-gather(bf16[2,4,768]{2,0,1:T(2,128)(2,1)S(1)} %copy.49), channel_id=1, replica_groups=mesh['row'=4,'col'=8] {'col'}, dimensions={1}, use_global_device_ids=true | all-gather | bytes 110592 | tf_op jit(solution)/shard_map/all_gather | solution.py:132
  59.7 2.6 fusion.63
  64.6 3.3 %fusion.32 = f32[12,64,64]{2,1,0:T(8,128)} fusion(bf16[512,12,64]{0,2,1:T(8,128)(2,1)} %bitcast.91, f32[12,512,64]{1,2,0:T(8,128)S(1)} %fusion.42, f32[12,512,64]{1,2,0:T(8,128)} %fusion.63, bf16[12,512,64]{1,2,0:T(8,128)(2,1)S(1)} %bitcast.81, bf16[12,64,512]{2,1,0:T(8,128)(2,1)} %convolution_convert_fusion.7), kind=kOutput, calls=%fused_computation.86 | convolution fusion | flops 53090368 | bytes 5701632 | tf_op jit(solution)/shard_map/while/body/eval_jaxpr/hqk,qhd->khd/dot_general | solution.py:103
  67.9 3.3 %convolution_convert_fusion.6 = bf16[12,64,512]{2,1,0:T(8,128)(2,1)} fusion(bf16[64,12,64]{0,2,1:T(8,128)(2,1)} %bitcast.103, f32[12,512,64]{1,2,0:T(8,128)S(1)} %fusion.42, f32[12,512,64]{1,2,0:T(8,128)} %fusion.63, bf16[12,512,64]{1,2,0:T(8,128)(2,1)S(1)} %bitcast.82, bf16[12,64,512]{2,1,0:T(8,128)(2,1)} %convolution_convert_fusion.7), kind=kOutput, calls=%fused_computation.74 | convolution fusion | flops 53483584 | bytes 5603328 | tf_op jit(solution)/shard_map/while/body/eval_jaxpr/hqk,khd->qhd/dot_general | solution.py:100
  71.2 2.8 fusion.62
  84.1 2.9 copy.57
  89.1 42.7 %all-reduce.6.cloned.1.call-done = bf16[2,32,768]{2,1,0:T(8,128)(2,1)} async-done(((bf16[2,32,768]{2,1,0:T(8,128)(2,1)}), bf16[2,32,768]{2,1,0:T(8,128)(2,1)}) %all-reduce.6.cloned.1.call-update) | async-done | bytes 98320
  133.8 6.3 %fusion.16 = (bf16[768]{0:T(1024)(128)(2,1)S(1)}, bf16[768]{0:T(1024)(128)(2,1)S(1)}, bf16[768]{0:T(1024)(128)(2,1)S(1)}, bf16[768]{0:T(1024)(128)(2,1)S(1)}, bf...) fusion(bf16[18,1,768]{2,1,0:T(2,128)(2,1)} %collective-permute-, ...), kind=kOutput, calls=%fused_computation.36 | convolution fusion | flops 625599744 | bytes 8523264 | tf_op jit(solution)/shard_map/dot_general | solution.py:38
  145.4 2.6 stack.49
  149.7 4.3 %pad_maximum_fusion = bf16[768,3072]{0,1:T(8,128)(2,1)} fusion(bf16[768,768]{0,1:T(8,128)(2,1)} %convolution_convert_fusion.1, bf16[768,768]{0,1:T(8,128)(2,1)S(1)} %copy-done.1, bf16[768,768]{0,1:T(8,128)(2,1)S(1)} %copy-done.2, bf16[768,768]{0,1:T(8,128)(2,1)} %convolution_convert_fusion), kind=kLoop, calls=%fused_computation.1 | loop fusion | flops 18874368 | bytes 9437184 | tf_op jit(solution)/shard_map/concatenate | solution.py:197
  156.5 4.5 %collective-permute-start.4 = (bf16[1,32,768]{2,1,0:T(8,128)(2,1)S(1)}, bf16[1,32,768]{2,1,0:T(8,128)(2,1)S(1)}, u32[]{:S(2)}, u32[]{:S(2)}) collective-permute-start(bf16[1,32,768]{2,1,0:T(8,128)(2,1)S(1)} %get-tuple-element.76), channel_id=1, source_target_pairs={{0,8},{8,16},{16,24},{1,9},{9,17},{17,25},{2,10},{10,18},{18,26},{... | collective-permute-start | bytes 147464 | tf_op jit(solution)/shard_map/ppermute | solution.py:22
  164.2 3.0 %collective-permute-start.6 = (bf16[18,1,768]{2,1,0:T(2,128)(2,1)S(1)}, bf16[18,1,768]{2,1,0:T(2,128)(2,1)S(1)}, u32[]{:S(2)}, u32[]{:S(2)}) collective-permute-start(bf16[18,1,768]{2,1,0:T(2,128)(2,1)S(1)} %get-tuple-element.72), channel_id=1, source_target_pairs={{0,1},{1,2},{2,3},{3,4},{4,5},{5,6},{6,7},{8,9},{9,10},{10,11},{11... | collective-permute-start | bytes 82952 | tf_op jit(solution)/shard_map/ppermute | solution.py:22
  167.2 15.0 %reduce-scatter.8.cloned.1.call-done = bf16[96,9]{1,0:T(8,128)(2,1)} async-done(((bf16[768,9]{1,0:T(8,128)(2,1)}), bf16[96,9]{1,0:T(8,128)(2,1)}) %reduce-scatter.8.cloned.1.call-update) | async-done | bytes 1744
  183.0 9.8 %psum.15 = bf16[9,96]{1,0:T(8,128)(2,1)S(1)} all-reduce(bf16[9,96]{1,0:T(8,128)(2,1)S(1)} %copy.70), channel_id=1, replica_groups=mesh['row'=4,'col'=8] {'row'}, use_global_device_ids=true, to_apply=%region_19.20 | all-reduce | flops 864 | bytes 3456 | tf_op jit(solution)/shard_map/psum | solution.py:208
  193.4 44.2 %reduce-scatter.6.cloned.1.call-done = bf16[768,384]{0,1:T(8,128)(2,1)} async-done(((bf16[768,3072]{0,1:T(8,128)(2,1)}), bf16[768,384]{0,1:T(8,128)(2,1)}) %reduce-scatter.6.cloned.1.call-update) | async-done | bytes 589840 | tf_op jit(solution)/shard_map/reduce_scatter | solution.py:199
  239.1 2.6 fusion.20
  241.6 43.3 %all-reduce.4.cloned.1.call-done = bf16[768,384]{0,1:T(8,128)(2,1)} async-done(((bf16[768,384]{0,1:T(8,128)(2,1)}), bf16[768,384]{0,1:T(8,128)(2,1)}) %all-reduce.4.cloned.1.call-update) | async-done | bytes 589840 | tf_op jit(solution)/shard_map/psum | solution.py:207
  285.0 2.3 copy.58
  (138 shorter events, 48.4 us)
Async XLA Ops:
  7.2 26.9 %copy-start = (bf16[768,768]{1,0:T(8,128)(2,1)S(1)}, bf16[768,768]{1,0:T(8,128)(2,1)}, u32[]{:S(2)}) copy-start(bf16[768,768]{1,0:T(8,128)(2,1)} %param.9) | copy-start | bytes 3538948
  7.2 124.6 %all-reduce.6.cloned.1.call-start = ((), (), s32[]{:S(2)}) async-start(), calls=%async_computation.5 | async-start | bytes 196608
  8.1 8.6 %collective-permute-start = (bf16[1,32,768]{2,1,0:T(8,128)(2,1)S(1)}, bf16[1,32,768]{2,1,0:T(8,128)(2,1)S(1)}, u32[]{:S(2)}, u32[]{:S(2)}) collective-permute-start(bf16[1,32,768]{2,1,0:T(8,128)(2,1)S(1)} %get-tuple-element.78), channel_id=1, source_target_pairs={{0,8},{8,16},{16,24},{1,9},{9,17},{17,25},{2,10},{10,18},{18,26},{... | collective-permute-start | bytes 147464 | tf_op jit(solution)/shard_map/ppermute | solution.py:22
  13.0 6.0 %collective-permute-start.1 = (bf16[1,32,768]{2,1,0:T(8,128)(2,1)S(1)}, bf16[1,32,768]{2,1,0:T(8,128)(2,1)S(1)}, u32[]{:S(2)}, u32[]{:S(2)}) collective-permute-start(bf16[1,32,768]{2,1,0:T(8,128)(2,1)S(1)} %get-tuple-element.79), channel_id=1, source_target_pairs={{8,0},{16,8},{24,16},{9,1},{17,9},{25,17},{10,2},{18,10},{26,18},{... | collective-permute-start | bytes 147464 | tf_op jit(solution)/shard_map/ppermute | solution.py:24
  16.7 8.1 %copy-start.33 = (f32[9,768]{1,0:T(8,128)S(1)}, f32[9,768]{1,0:T(8,128)}, u32[]{:S(2)}) copy-start(f32[9,768]{1,0:T(8,128)} %param.8) | copy-start | bytes 82948
  16.7 8.8 %copy-start.22 = (bf16[1,32,768]{2,1,0:T(8,128)(2,1)}, bf16[1,32,768]{2,1,0:T(8,128)(2,1)S(1)}, u32[]{:S(2)}) copy-start(bf16[1,32,768]{2,1,0:T(8,128)(2,1)S(1)} %collective-permute-done) | copy-start | bytes 147460
  19.0 6.5 %copy-start.23 = (bf16[1,32,768]{2,1,0:T(8,128)(2,1)}, bf16[1,32,768]{2,1,0:T(8,128)(2,1)S(1)}, u32[]{:S(2)}) copy-start(bf16[1,32,768]{2,1,0:T(8,128)(2,1)S(1)} %collective-permute-done.1) | copy-start | bytes 147460
  19.0 6.5 %copy-start.17 = (bf16[18,32,768]{2,1,0:T(8,128)(2,1)}, bf16[18,32,768]{2,1,0:T(8,128)(2,1)S(1)}, u32[]{:S(2)}) copy-start(bf16[18,32,768]{2,1,0:T(8,128)(2,1)S(1)} %constant_dynamic-update-slice_fusion) | copy-start | bytes 2654212
  19.9 7.8 %collective-permute-start.3 = (bf16[18,1,768]{2,1,0:T(2,128)(2,1)}, bf16[18,1,768]{2,1,0:T(2,128)(2,1)}, u32[]{:S(2)}, u32[]{:S(2)}) collective-permute-start(bf16[18,1,768]{2,1,0:T(2,128)(2,1)} %get-tuple-element.74), channel_id=1, source_target_pairs={{1,0},{2,1},{3,2},{4,3},{5,4},{6,5},{7,6},{9,8},{10,9},{11,10},{12... | collective-permute-start | bytes 82952 | tf_op jit(solution)/shard_map/ppermute | solution.py:24
  21.2 6.5 %collective-permute-start.2 = (bf16[18,1,768]{2,1,0:T(2,128)(2,1)}, bf16[18,1,768]{2,1,0:T(2,128)(2,1)}, u32[]{:S(2)}, u32[]{:S(2)}) collective-permute-start(bf16[18,1,768]{2,1,0:T(2,128)(2,1)} %get-tuple-element.75), channel_id=1, source_target_pairs={{0,1},{1,2},{2,3},{3,4},{4,5},{5,6},{6,7},{8,9},{9,10},{10,11},{11... | collective-permute-start | bytes 82952 | tf_op jit(solution)/shard_map/ppermute | solution.py:22
  35.7 18.5 %copy-start.3 = (bf16[768,768]{1,0:T(8,128)(2,1)S(1)}, bf16[768,768]{1,0:T(8,128)(2,1)}, u32[]{:S(2)}) copy-start(bf16[768,768]{1,0:T(8,128)(2,1)} %param.10) | copy-start | bytes 3538948
  71.2 4.9 %copy-start.4 = (bf16[768,768]{1,0:T(8,128)(2,1)S(1)}, bf16[768,768]{1,0:T(8,128)(2,1)}, u32[]{:S(2)}) copy-start(bf16[768,768]{1,0:T(8,128)(2,1)} %param.11) | copy-start | bytes 3538948
  78.0 104.2 %reduce-scatter.8.cloned.1.call-start = ((), (), s32[]{:S(2)}) async-start(), calls=%async_computation.4 | async-start | bytes 221184
  87.0 44.7 %copy-start.21 = (f32[2,4,768]{2,1,0:T(4,128)S(1)}, f32[2,4,768]{2,1,0:T(4,128)}, u32[]{:S(2)}) copy-start(f32[2,4,768]{2,1,0:T(4,128)} %copy-done.20) | copy-start | bytes 73732
  87.0 44.7 %copy-start.30 = (f32[2,4]{1,0:T(2,128)S(1)}, f32[2,4]{1,0:T(2,128)}, u32[]{:S(2)}) copy-start(f32[2,4]{1,0:T(2,128)} %copy-done.29) | copy-start | bytes 100
  87.1 44.7 %copy-start.32 = (f32[2,4]{1,0:T(2,128)S(1)}, f32[2,4]{1,0:T(2,128)}, u32[]{:S(2)}) copy-start(f32[2,4]{1,0:T(2,128)} %copy-done.31) | copy-start | bytes 100
  133.8 15.9 %copy-start.1 = (bf16[768,768]{0,1:T(8,128)(2,1)S(1)}, bf16[768,768]{0,1:T(8,128)(2,1)}, u32[]{:S(2)}) copy-start(bf16[768,768]{0,1:T(8,128)(2,1)} %convolution_convert_fusion.2) | copy-start | bytes 3538948
  133.8 15.9 %copy-start.2 = (bf16[768,768]{0,1:T(8,128)(2,1)S(1)}, bf16[768,768]{0,1:T(8,128)(2,1)}, u32[]{:S(2)}) copy-start(bf16[768,768]{0,1:T(8,128)(2,1)} %convolution_convert_fusion.3) | copy-start | bytes 3538948
  149.7 87.9 %reduce-scatter.6.cloned.1.call-start = ((), (), s32[]{:S(2)}) async-start(), calls=%async_computation.2 | async-start | bytes 5308416 | tf_op jit(solution)/shard_map/reduce_scatter | solution.py:199
  154.1 130.9 %all-reduce.4.cloned.1.call-start = ((), (), s32[]{:S(2)}) async-start(), calls=%async_computation.3 | async-start | bytes 1179648 | tf_op jit(solution)/shard_map/psum | solution.py:207
  155.2 6.0 %collective-permute-start.5 = (bf16[1,32,768]{2,1,0:T(8,128)(2,1)S(1)}, bf16[1,32,768]{2,1,0:T(8,128)(2,1)S(1)}, u32[]{:S(2)}, u32[]{:S(2)}) collective-permute-start(bf16[1,32,768]{2,1,0:T(8,128)(2,1)S(1)} %get-tuple-element.77), channel_id=1, source_target_pairs={{8,0},{16,8},{24,16},{9,1},{17,9},{25,17},{10,2},{18,10},{26,18},{... | collective-permute-start | bytes 147464 | tf_op jit(solution)/shard_map/ppermute | solution.py:24
  156.5 6.3 %collective-permute-start.4 = (bf16[1,32,768]{2,1,0:T(8,128)(2,1)S(1)}, bf16[1,32,768]{2,1,0:T(8,128)(2,1)S(1)}, u32[]{:S(2)}, u32[]{:S(2)}) collective-permute-start(bf16[1,32,768]{2,1,0:T(8,128)(2,1)S(1)} %get-tuple-element.76), channel_id=1, source_target_pairs={{0,8},{8,16},{16,24},{1,9},{9,17},{17,25},{2,10},{10,18},{18,26},{... | collective-permute-start | bytes 147464 | tf_op jit(solution)/shard_map/ppermute | solution.py:22
  162.9 74.8 %collective-permute-start.7 = (bf16[18,1,768]{2,1,0:T(2,128)(2,1)S(1)}, bf16[18,1,768]{2,1,0:T(2,128)(2,1)S(1)}, u32[]{:S(2)}, u32[]{:S(2)}) collective-permute-start(bf16[18,1,768]{2,1,0:T(2,128)(2,1)S(1)} %get-tuple-element.73), channel_id=1, source_target_pairs={{1,0},{2,1},{3,2},{4,3},{5,4},{6,5},{7,6},{9,8},{10,9},{11,10},{12... | collective-permute-start | bytes 82952 | tf_op jit(solution)/shard_map/ppermute | solution.py:24
  164.2 73.5 %collective-permute-start.6 = (bf16[18,1,768]{2,1,0:T(2,128)(2,1)S(1)}, bf16[18,1,768]{2,1,0:T(2,128)(2,1)S(1)}, u32[]{:S(2)}, u32[]{:S(2)}) collective-permute-start(bf16[18,1,768]{2,1,0:T(2,128)(2,1)S(1)} %get-tuple-element.72), channel_id=1, source_target_pairs={{0,1},{1,2},{2,3},{3,4},{4,5},{5,6},{6,7},{8,9},{9,10},{10,11},{11... | collective-permute-start | bytes 82952 | tf_op jit(solution)/shard_map/ppermute | solution.py:22
  (23 other events, 44.4 us)
Sparse Core Ops, SparseCore 0:
  78.2 53.5 all-reduce.5
  149.8 32.3 reduce-scatter.7
  184.5 53.0 reduce-scatter.5
  240.5 44.4 all-reduce.3
where the time goes:
time: 295 us; the launch traced here: 294 us
  waiting for transfers between devices  149 us (51%)
  matrix products  38.1 us (13%)
  local copies, waits for them, and re-layouts  29.3 us (10%)
  blocking collectives  23.8 us (8%)
  starting transfers between devices  21.6 us (7%)
  other arithmetic  16.9 us (6%)
  between operations  14.9 us (5%)
    unnamed x6, waiting for transfers between devices  57.7 us
    reduce_scatter x1, waiting for transfers between devices, on_device(): lax.psum_scatter(weight_terms.astype(jnp.bfloat16), 'col', scatter_dimens...  44.2 us
    psum x1, waiting for transfers between devices, on_device(): lax.psum(column_sums[0].astype(jnp.bfloat16), 'row').astype(jnp.float32)  43.3 us
    ppermute x4, starting transfers between devices, with_halo(): lax.ppermute(tail, axis, [(i, (i + 1) % count) for i in range(ends)])  16.1 us
    all_gather x1, blocking collectives, on_device(): gathered = lax.all_gather(normed, 'col', axis=1, tiled=True)  14 us
    psum x1, blocking collectives, on_device(): lax.psum(column_sums[1].astype(jnp.bfloat16), 'row').astype(jnp.float32)  9.8 us
    unnamed x76, local copies, waits for them, and re-layouts  9.51 us
    dot_general x2, matrix products, contract_last(): lax.dot_general(left, right, (((1,), (1,)), ((), ())), preferred_element_...  8.7 us
  transfers between devices with their start and end apart: 12, of which 7 were waited for; matrix products, arithmetic and copies ran while one was open for 8% of the time, Pallas kernels for 0%

commit v1 on v0

--- a/solution.py
+++ b/solution.py
@@ -204,7 +204,9 @@
         ).astype(jnp.float32),
     )
     grad_weights, grad_conv = (
-        lax.psum(column_sums[0].astype(jnp.bfloat16), "row").astype(jnp.float32),
+        jnp.sum(lax.all_gather(column_sums[0].astype(jnp.bfloat16), "row"), axis=0).astype(
+            jnp.float32
+        ),
         lax.psum(column_sums[1].astype(jnp.bfloat16), "row").astype(jnp.float32),
     )
     return (grad_image, grad_weights, grad_conv)

time: 295 us -> 278 us (0.942)
  waiting for transfers between devices: 149 us -> 136 us
  local copies, waits for them, and re-layouts: 29.3 us -> 24 us
    psum x1 -> x0, waiting for transfers between devices: 43.3 us -> none  [on_device(): lax.psum(column_sums[0].astype(jnp.bfloat16), 'row').astype(jnp.float32)]
    all_gather x0 -> x1, waiting for transfers between devices: none -> 21.9 us  [on_device(): lax.all_gather(column_sums[0].astype(jnp.bfloat16), 'row')]
    another operation x10, local copies, waits for them, and re-layouts: 7.91 us -> 0.12 us  [on_device(): tap_terms = jnp.stack(tap_list, axis=0)]
    reduce_scatter x1, waiting for transfers between devices: 44.2 us -> 49.6 us  [on_device(): lax.psum_scatter(weight_terms.astype(jnp.bfloat16), 'col', scatter_dimens...]
    all_gather x0 -> x1, local copies, waits for them, and re-layouts: none -> 4.52 us  [on_device(): lax.all_gather(column_sums[0].astype(jnp.bfloat16), 'row')]
    reduce_sum x0 -> x1, other arithmetic: none -> 4 us  [on_device(): jnp.sum(lax.all_gather(column_sums[0].astype(jnp.bfloat16), 'row'), axis=0)]
    unnamed x6, waiting for transfers between devices: 57.7 us -> 61.1 us
    unnamed x76 -> x72, local copies, waits for them, and re-layouts: 9.51 us -> 7.43 us
  transfers between devices with their start and end apart: 12 -> 12, of which waited for: 7 -> 7; matrix products, arithmetic and copies ran while one was open for 8% -> 10% of each run, Pallas kernels for 0% -> 0%
where the time goes in v1:
time: 278 us; the launch traced here: 277 us
  waiting for transfers between devices  136 us (49%)
  matrix products  35.2 us (13%)
  blocking collectives  26 us (9%)
  local copies, waits for them, and re-layouts  24 us (9%)
  starting transfers between devices  21.6 us (8%)
  other arithmetic  18.7 us (7%)
  between operations  15 us (5%)
    unnamed x6, waiting for transfers between devices  61.1 us
    reduce_scatter x1, waiting for transfers between devices, on_device(): lax.psum_scatter(weight_terms.astype(jnp.bfloat16), 'col', scatter_dimens...  49.6 us
    all_gather x1, waiting for transfers between devices, on_device(): lax.all_gather(column_sums[0].astype(jnp.bfloat16), 'row')  21.9 us
    ppermute x4, starting transfers between devices, with_halo(): lax.ppermute(tail, axis, [(i, (i + 1) % count) for i in range(ends)])  16.1 us
    all_gather x1, blocking collectives, on_device(): gathered = lax.all_gather(normed, 'col', axis=1, tiled=True)  16.1 us
    psum x1, blocking collectives, on_device(): lax.psum(column_sums[1].astype(jnp.bfloat16), 'row').astype(jnp.float32)  9.92 us
    dot_general x2, matrix products, contract_last(): lax.dot_general(left, right, (((1,), (1,)), ((), ())), preferred_element_...  8.45 us
    unnamed x72, local copies, waits for them, and re-layouts  7.43 us
  transfers between devices with their start and end apart: 12, of which 7 were waited for; matrix products, arithmetic and copies ran while one was open for 10% of the time, Pallas kernels for 0%

profile of v1, /device:TPU:0, one launch (start us, length us, event | category | flops | bytes accessed | tf_op | source)
XLA Modules:
  0.0 277.1 jit_solution(15146009227457146195)
XLA Ops:
  8.1 4.9 %collective-permute-start = (bf16[1,32,768]{2,1,0:T(8,128)(2,1)S(1)}, bf16[1,32,768]{2,1,0:T(8,128)(2,1)S(1)}, u32[]{:S(2)}, u32[]{:S(2)}) collective-permute-start(bf16[1,32,768]{2,1,0:T(8,128)(2,1)S(1)} %get-tuple-element.72), channel_id=1, source_target_pairs={{0,8},{8,16},{16,24},{1,9},{9,17},{17,25},{2,10},{10,18},{18,26},{... | collective-permute-start | bytes 147464 | tf_op jit(solution)/shard_map/ppermute | solution.py:22
  14.3 2.4 convolution_convert_fusion.4
  21.2 3.6 %collective-permute-start.2 = (bf16[18,1,768]{2,1,0:T(2,128)(2,1)}, bf16[18,1,768]{2,1,0:T(2,128)(2,1)}, u32[]{:S(2)}, u32[]{:S(2)}) collective-permute-start(bf16[18,1,768]{2,1,0:T(2,128)(2,1)} %get-tuple-element.69), channel_id=1, source_target_pairs={{0,1},{1,2},{2,3},{3,4},{4,5},{5,6},{6,7},{8,9},{9,10},{10,11},{11... | collective-permute-start | bytes 82952 | tf_op jit(solution)/shard_map/ppermute | solution.py:22
  25.9 5.1 %fusion.28 = bf16[16,32,768]{2,1,0:T(8,128)(2,1)S(1)} fusion(bf16[16,32,768]{2,1,0:T(8,128)(2,1)S(1)} %copy-done.3, bf16[1,32,768]{2,1,0:T(8,128)(2,1)} %copy-done.20, bf16[1,32,768]{2,1,0:T(8,128)(2,1)} %copy-done.18, f32[768]{0:T(1024)} %get-tuple-element.63, f32[768]{0:T(1024)} %get-tuple-element.64, f32[768]{0:T(1024)S(1)} %get-tuple-element.57, ...), kind=kLoop, calls=%fused_computation.62 | loop fusion | flops 20447232 | bytes 2638848 | tf_op jit(solution)/shard_map/convert_element_type | solution.py:119
  33.5 2.4 copy.49
  38.1 16.1 %all_gather.9 = bf16[2,32,768]{2,0,1:T(2,128)(2,1)S(1)} all-gather(bf16[2,4,768]{2,0,1:T(2,128)(2,1)S(1)} %copy.47), channel_id=1, replica_groups=mesh['row'=4,'col'=8] {'col'}, dimensions={1}, use_global_device_ids=true | all-gather | bytes 110592 | tf_op jit(solution)/shard_map/all_gather | solution.py:132
  59.6 2.6 fusion.63
  64.5 3.3 %fusion.32 = f32[12,64,64]{2,1,0:T(8,128)} fusion(bf16[512,12,64]{0,2,1:T(8,128)(2,1)} %bitcast.93, f32[12,512,64]{1,2,0:T(8,128)S(1)} %fusion.42, f32[12,512,64]{1,2,0:T(8,128)} %fusion.63, bf16[12,512,64]{1,2,0:T(8,128)(2,1)S(1)} %bitcast.83, bf16[12,64,512]{2,1,0:T(8,128)(2,1)} %convolution_convert_fusion.7), kind=kOutput, calls=%fused_computation.86 | convolution fusion | flops 53090368 | bytes 5701632 | tf_op jit(solution)/shard_map/while/body/eval_jaxpr/hqk,qhd->khd/dot_general | solution.py:103
  67.8 3.3 %convolution_convert_fusion.6 = bf16[12,64,512]{2,1,0:T(8,128)(2,1)} fusion(bf16[64,12,64]{0,2,1:T(8,128)(2,1)} %bitcast.105, f32[12,512,64]{1,2,0:T(8,128)S(1)} %fusion.42, f32[12,512,64]{1,2,0:T(8,128)} %fusion.63, bf16[12,512,64]{1,2,0:T(8,128)(2,1)S(1)} %bitcast.84, bf16[12,64,512]{2,1,0:T(8,128)(2,1)} %convolution_convert_fusion.7), kind=kOutput, calls=%fused_computation.74 | convolution fusion | flops 53483584 | bytes 5603328 | tf_op jit(solution)/shard_map/while/body/eval_jaxpr/hqk,khd->qhd/dot_general | solution.py:100
  71.1 2.7 fusion.62
  81.1 2.5 pad_maximum_fusion
  85.6 2.9 %copy.55 = bf16[512,12,64]{2,1,0:T(8,128)(2,1)S(1)} copy(bf16[512,12,64]{0,2,1:T(8,128)(2,1)} %bitcast.94) | data formatting | bytes 1572864 | tf_op jit(solution)/shard_map/while/body/eval_jaxpr/convert_element_type | solution.py:102
  90.6 41.0 %all-reduce.3.cloned.1.call-done = bf16[2,32,768]{2,1,0:T(8,128)(2,1)} async-done(((bf16[2,32,768]{2,1,0:T(8,128)(2,1)}), bf16[2,32,768]{2,1,0:T(8,128)(2,1)}) %all-reduce.3.cloned.1.call-update) | async-done | bytes 98320
  133.6 6.1 %fusion.16 = (bf16[768]{0:T(1024)(128)(2,1)S(1)}, bf16[768]{0:T(1024)(128)(2,1)S(1)}, bf16[768]{0:T(1024)(128)(2,1)S(1)}, bf16[768]{0:T(1024)(128)(2,1)S(1)}, bf...) fusion(bf16[18,1,768]{2,1,0:T(2,128)(2,1)} %collective-permute-, ...), kind=kOutput, calls=%fused_computation.36 | convolution fusion | flops 625599744 | bytes 8523264 | tf_op jit(solution)/shard_map/dot_general | solution.py:38
  140.7 49.6 %reduce-scatter.6.cloned.1.call-done = bf16[768,384]{0,1:T(8,128)(2,1)} async-done(((bf16[768,3072]{0,1:T(8,128)(2,1)}), bf16[768,384]{0,1:T(8,128)(2,1)}) %reduce-scatter.6.cloned.1.call-update) | async-done | bytes 589840 | tf_op jit(solution)/shard_map/reduce_scatter | solution.py:199
  191.7 4.5 %collective-permute-start.4 = (bf16[1,32,768]{2,1,0:T(8,128)(2,1)S(1)}, bf16[1,32,768]{2,1,0:T(8,128)(2,1)S(1)}, u32[]{:S(2)}, u32[]{:S(2)}) collective-permute-start(bf16[1,32,768]{2,1,0:T(8,128)(2,1)S(1)} %get-tuple-element.70), channel_id=1, source_target_pairs={{0,8},{8,16},{16,24},{1,9},{9,17},{17,25},{2,10},{10,18},{18,26},{... | collective-permute-start | bytes 147464 | tf_op jit(solution)/shard_map/ppermute | solution.py:22
  199.4 3.0 %collective-permute-start.6 = (bf16[18,1,768]{2,1,0:T(2,128)(2,1)S(1)}, bf16[18,1,768]{2,1,0:T(2,128)(2,1)S(1)}, u32[]{:S(2)}, u32[]{:S(2)}) collective-permute-start(bf16[18,1,768]{2,1,0:T(2,128)(2,1)S(1)} %get-tuple-element.66), channel_id=1, source_target_pairs={{0,1},{1,2},{2,3},{3,4},{4,5},{5,6},{6,7},{8,9},{9,10},{10,11},{11... | collective-permute-start | bytes 82952 | tf_op jit(solution)/shard_map/ppermute | solution.py:22
  202.4 20.1 %reduce-scatter.8.cloned.1.call-done = bf16[96,9]{1,0:T(8,128)(2,1)} async-done(((bf16[768,9]{1,0:T(8,128)(2,1)}), bf16[96,9]{1,0:T(8,128)(2,1)}) %reduce-scatter.8.cloned.1.call-update) | async-done | bytes 1744
  223.3 9.9 %psum.7 = bf16[9,96]{1,0:T(8,128)(2,1)S(1)} all-reduce(bf16[9,96]{1,0:T(8,128)(2,1)S(1)} %copy.68), channel_id=1, replica_groups=mesh['row'=4,'col'=8] {'row'}, use_global_device_ids=true, to_apply=%region_19.20 | all-reduce | flops 864 | bytes 3456 | tf_op jit(solution)/shard_map/psum | solution.py:210
  235.2 2.6 fusion.20
  237.8 21.9 %all-gather.3.cloned.1.call-done = bf16[3072,384]{0,1:T(8,128)(2,1)} async-done(((bf16[768,384]{0,1:T(8,128)(2,1)}), bf16[3072,384]{0,1:T(8,128)(2,1)}) %all-gather.3.cloned.1.call-update) | async-done | bytes 2359312 | tf_op jit(solution)/shard_map/all_gather | solution.py:207
  259.7 4.5 %reshape.111 = bf16[4,768,384]{1,0,2:T(4,128)(2,1)S(1)} reshape(bf16[3072,384]{0,1:T(8,128)(2,1)} %all-gather.3.cloned.1.call-done) | data formatting | bytes 4718592 | tf_op jit(solution)/shard_map/all_gather | solution.py:207
  264.2 4.0 %reduce_sum.154 = bf16[768,384]{0,1:T(8,128)(2,1)} reduce(bf16[4,768,384]{1,0,2:T(4,128)(2,1)S(1)} %reshape.111, bf16[]{:T(256)} %constant.33.clone.1), dimensions={0}, to_apply=%region_8.9 | reduce | flops 884736 | bytes 2949122 | tf_op jit(solution)/shard_map/reduce_sum | solution.py:207
  268.2 2.3 copy.56
  (136 shorter events, 40.7 us)
Async XLA Ops:
  7.2 24.7 %copy-start = (bf16[768,768]{1,0:T(8,128)(2,1)S(1)}, bf16[768,768]{1,0:T(8,128)(2,1)}, u32[]{:S(2)}) copy-start(bf16[768,768]{1,0:T(8,128)(2,1)} %param.9) | copy-start | bytes 3538948
  7.2 124.4 %all-reduce.3.cloned.1.call-start = ((), (), s32[]{:S(2)}) async-start(), calls=%async_computation.5 | async-start | bytes 196608
  8.1 8.6 %collective-permute-start = (bf16[1,32,768]{2,1,0:T(8,128)(2,1)S(1)}, bf16[1,32,768]{2,1,0:T(8,128)(2,1)S(1)}, u32[]{:S(2)}, u32[]{:S(2)}) collective-permute-start(bf16[1,32,768]{2,1,0:T(8,128)(2,1)S(1)} %get-tuple-element.72), channel_id=1, source_target_pairs={{0,8},{8,16},{16,24},{1,9},{9,17},{17,25},{2,10},{10,18},{18,26},{... | collective-permute-start | bytes 147464 | tf_op jit(solution)/shard_map/ppermute | solution.py:22
  13.0 6.0 %collective-permute-start.1 = (bf16[1,32,768]{2,1,0:T(8,128)(2,1)S(1)}, bf16[1,32,768]{2,1,0:T(8,128)(2,1)S(1)}, u32[]{:S(2)}, u32[]{:S(2)}) collective-permute-start(bf16[1,32,768]{2,1,0:T(8,128)(2,1)S(1)} %get-tuple-element.73), channel_id=1, source_target_pairs={{8,0},{16,8},{24,16},{9,1},{17,9},{25,17},{10,2},{18,10},{26,18},{... | collective-permute-start | bytes 147464 | tf_op jit(solution)/shard_map/ppermute | solution.py:24
  16.7 8.2 %copy-start.31 = (f32[9,768]{1,0:T(8,128)S(1)}, f32[9,768]{1,0:T(8,128)}, u32[]{:S(2)}) copy-start(f32[9,768]{1,0:T(8,128)} %param.8) | copy-start | bytes 82948
  16.7 8.1 %copy-start.18 = (bf16[1,32,768]{2,1,0:T(8,128)(2,1)}, bf16[1,32,768]{2,1,0:T(8,128)(2,1)S(1)}, u32[]{:S(2)}) copy-start(bf16[1,32,768]{2,1,0:T(8,128)(2,1)S(1)} %collective-permute-done) | copy-start | bytes 147460
  19.0 5.9 %copy-start.20 = (bf16[1,32,768]{2,1,0:T(8,128)(2,1)}, bf16[1,32,768]{2,1,0:T(8,128)(2,1)S(1)}, u32[]{:S(2)}) copy-start(bf16[1,32,768]{2,1,0:T(8,128)(2,1)S(1)} %collective-permute-done.1) | copy-start | bytes 147460
  19.0 5.9 %copy-start.14 = (bf16[18,32,768]{2,1,0:T(8,128)(2,1)}, bf16[18,32,768]{2,1,0:T(8,128)(2,1)S(1)}, u32[]{:S(2)}) copy-start(bf16[18,32,768]{2,1,0:T(8,128)(2,1)S(1)} %constant_dynamic-update-slice_fusion) | copy-start | bytes 2654212
  19.9 5.9 %collective-permute-start.3 = (bf16[18,1,768]{2,1,0:T(2,128)(2,1)}, bf16[18,1,768]{2,1,0:T(2,128)(2,1)}, u32[]{:S(2)}, u32[]{:S(2)}) collective-permute-start(bf16[18,1,768]{2,1,0:T(2,128)(2,1)} %get-tuple-element.68), channel_id=1, source_target_pairs={{1,0},{2,1},{3,2},{4,3},{5,4},{6,5},{7,6},{9,8},{10,9},{11,10},{12... | collective-permute-start | bytes 82952 | tf_op jit(solution)/shard_map/ppermute | solution.py:24
  21.2 4.6 %collective-permute-start.2 = (bf16[18,1,768]{2,1,0:T(2,128)(2,1)}, bf16[18,1,768]{2,1,0:T(2,128)(2,1)}, u32[]{:S(2)}, u32[]{:S(2)}) collective-permute-start(bf16[18,1,768]{2,1,0:T(2,128)(2,1)} %get-tuple-element.69), channel_id=1, source_target_pairs={{0,1},{1,2},{2,3},{3,4},{4,5},{5,6},{6,7},{8,9},{9,10},{10,11},{11... | collective-permute-start | bytes 82952 | tf_op jit(solution)/shard_map/ppermute | solution.py:22
  33.5 20.7 %copy-start.1 = (bf16[768,768]{1,0:T(8,128)(2,1)S(1)}, bf16[768,768]{1,0:T(8,128)(2,1)}, u32[]{:S(2)}) copy-start(bf16[768,768]{1,0:T(8,128)(2,1)} %param.10) | copy-start | bytes 3538948
  78.0 112.4 %reduce-scatter.6.cloned.1.call-start = ((), (), s32[]{:S(2)}) async-start(), calls=%async_computation.2 | async-start | bytes 5308416 | tf_op jit(solution)/shard_map/reduce_scatter | solution.py:199
  83.7 138.8 %reduce-scatter.8.cloned.1.call-start = ((), (), s32[]{:S(2)}) async-start(), calls=%async_computation.4 | async-start | bytes 221184
  88.5 43.1 %copy-start.17 = (f32[2,4,768]{2,1,0:T(4,128)S(1)}, f32[2,4,768]{2,1,0:T(4,128)}, u32[]{:S(2)}) copy-start(f32[2,4,768]{2,1,0:T(4,128)} %copy-done.16) | copy-start | bytes 73732
  88.5 43.1 %copy-start.28 = (f32[2,4]{1,0:T(2,128)S(1)}, f32[2,4]{1,0:T(2,128)}, u32[]{:S(2)}) copy-start(f32[2,4]{1,0:T(2,128)} %copy-done.27) | copy-start | bytes 100
  88.5 43.0 %copy-start.30 = (f32[2,4]{1,0:T(2,128)S(1)}, f32[2,4]{1,0:T(2,128)}, u32[]{:S(2)}) copy-start(f32[2,4]{1,0:T(2,128)} %copy-done.29) | copy-start | bytes 100
  88.5 45.0 %copy-start.19 = (bf16[1,32,768]{2,1,0:T(8,128)(2,1)S(1)}, bf16[1,32,768]{2,1,0:T(8,128)(2,1)}, u32[]{:S(2)}) copy-start(bf16[1,32,768]{2,1,0:T(8,128)(2,1)} %copy-done.18) | copy-start | bytes 147460
  88.5 45.0 %copy-start.21 = (bf16[1,32,768]{2,1,0:T(8,128)(2,1)S(1)}, bf16[1,32,768]{2,1,0:T(8,128)(2,1)}, u32[]{:S(2)}) copy-start(bf16[1,32,768]{2,1,0:T(8,128)(2,1)} %copy-done.20) | copy-start | bytes 147460
  90.6 43.0 %copy-start.4 = (bf16[16,32,768]{2,1,0:T(8,128)(2,1)S(1)}, bf16[16,32,768]{2,1,0:T(8,128)(2,1)}, u32[]{:S(2)}) copy-start(bf16[16,32,768]{2,1,0:T(8,128)(2,1)} %param.7) | copy-start | bytes 2359300
  140.7 119.0 %all-gather.3.cloned.1.call-start = ((), (), s32[]{:S(2)}) async-start(), calls=%async_computation.3 | async-start | bytes 2949120 | tf_op jit(solution)/shard_map/all_gather | solution.py:207
  190.4 6.0 %collective-permute-start.5 = (bf16[1,32,768]{2,1,0:T(8,128)(2,1)S(1)}, bf16[1,32,768]{2,1,0:T(8,128)(2,1)S(1)}, u32[]{:S(2)}, u32[]{:S(2)}) collective-permute-start(bf16[1,32,768]{2,1,0:T(8,128)(2,1)S(1)} %get-tuple-element.71), channel_id=1, source_target_pairs={{8,0},{16,8},{24,16},{9,1},{17,9},{25,17},{10,2},{18,10},{26,18},{... | collective-permute-start | bytes 147464 | tf_op jit(solution)/shard_map/ppermute | solution.py:24
  191.7 6.3 %collective-permute-start.4 = (bf16[1,32,768]{2,1,0:T(8,128)(2,1)S(1)}, bf16[1,32,768]{2,1,0:T(8,128)(2,1)S(1)}, u32[]{:S(2)}, u32[]{:S(2)}) collective-permute-start(bf16[1,32,768]{2,1,0:T(8,128)(2,1)S(1)} %get-tuple-element.70), channel_id=1, source_target_pairs={{0,8},{8,16},{16,24},{1,9},{9,17},{17,25},{2,10},{10,18},{18,26},{... | collective-permute-start | bytes 147464 | tf_op jit(solution)/shard_map/ppermute | solution.py:22
  198.1 35.8 %collective-permute-start.7 = (bf16[18,1,768]{2,1,0:T(2,128)(2,1)S(1)}, bf16[18,1,768]{2,1,0:T(2,128)(2,1)S(1)}, u32[]{:S(2)}, u32[]{:S(2)}) collective-permute-start(bf16[18,1,768]{2,1,0:T(2,128)(2,1)S(1)} %get-tuple-element.67), channel_id=1, source_target_pairs={{1,0},{2,1},{3,2},{4,3},{5,4},{6,5},{7,6},{9,8},{10,9},{11,10},{12... | collective-permute-start | bytes 82952 | tf_op jit(solution)/shard_map/ppermute | solution.py:24
  199.4 34.5 %collective-permute-start.6 = (bf16[18,1,768]{2,1,0:T(2,128)(2,1)S(1)}, bf16[18,1,768]{2,1,0:T(2,128)(2,1)S(1)}, u32[]{:S(2)}, u32[]{:S(2)}) collective-permute-start(bf16[18,1,768]{2,1,0:T(2,128)(2,1)S(1)} %get-tuple-element.66), channel_id=1, source_target_pairs={{0,1},{1,2},{2,3},{3,4},{4,5},{5,6},{6,7},{8,9},{9,10},{10,11},{11... | collective-permute-start | bytes 82952 | tf_op jit(solution)/shard_map/ppermute | solution.py:22
  (21 other events, 38.5 us)
Sparse Core Ops, SparseCore 0:
  78.1 53.4 all-reduce.2
  133.9 56.4 reduce-scatter.5
  193.2 29.2 reduce-scatter.7
  224.2 35.4 all-gather.2
